TPU v7x, 256 devices: a whole 4x4x8 slice. The times are simulated.
256 devices in a mesh: pipe: 4 (over y), expert: 16 (over z, core), dp: 4 (over x).
Axes of the slice: x: 4, y: 4, z: 8, core: 2. Of those that a mesh axis runs over, the one named last changes fastest.
Arguments:
- normed: bfloat16 [4, 4, 3072, 4096], P('pipe', None, ('expert', 'dp')), may hold values from -1.5 to 1.5
- saved_out: bfloat16 [4, 4, 3072, 2, 4096], P('pipe', None, ('expert', 'dp')), may hold values from -0.59765625 to 0.59765625
- expert_grads: bfloat16 [4, 4, 4, 16, 16, 9, 4096], P('pipe', None, 'dp', 'expert'), may hold values from -24 to 24
- routes: int32 [4, 4, 3072, 2], P('pipe', None, ('expert', 'dp')), may hold values from 0 to 15, all different within a row; in each aligned block of 48 rows (0 to 47, 48 to 95, ..., all dimensions but the last counted through in order) at most 9 rows name the same one
- router_weight: bfloat16 [4, 4096, 16], P('pipe'), may hold values from -0.375 to 0.375
- upstream: bfloat16 [4, 3072, 4096], P(None, ('expert', 'dp')), may hold values from -6 to 6
Outputs:
- grad_input: bfloat16 [4, 4, 3072, 4096], P('pipe', None, ('expert', 'dp'))
- router_grad: float32 [4, 4096, 16], P('pipe')
Inputs may be any that keep to these rules, and one draw needn't show every extreme that they name: `routes`: the two experts of a row differ. Within the 48 rows of one device for one section and micro-batch no expert is named more than 9 times, a bound that some expert reaches in some of these blocks.
All inputs are finite; a program needn't handle non-finite values.
Results may differ from a plain program's by a relative error of at most 0.007.
Values may be sent and summed in bfloat16 or wider, within the bound.
No kernel may reach another device: no remote copies, remote signals or barrier semaphores. Data moves between devices by JAX's collectives and lax.ppermute only.
A program may use at most 128 MiB of HBM per device.

v0:
```python
import jax
import jax.numpy as jnp
from jax import lax
from jax.sharding import PartitionSpec as P


def shifted(block, axis, distance):
    devices = range(lax.axis_size(axis))
    route = [(i - distance, i) for i in devices if i - distance in devices]
    return lax.ppermute(block, axis, route)


def slot_index(flat, experts, capacity):
    onehot = (flat[..., None] == jnp.arange(experts, dtype=jnp.int32)).astype(jnp.int32)
    before = jnp.cumsum(onehot, axis=-2) - onehot
    position = jnp.sum(before * onehot, axis=-1)
    return flat * capacity + position


def block_grad(incoming, normed_rows, saved_rows, route_rows, returned, index_rows, router_w):
    experts = router_w.shape[1]
    rows_dev = normed_rows.shape[0]
    width = normed_rows.shape[1]
    logits = jnp.dot(normed_rows, router_w, preferred_element_type=jnp.float32)
    expl = jnp.exp(logits)
    probs = expl / jnp.sum(expl, axis=-1, keepdims=True)
    chosen = (route_rows[..., None] == jnp.arange(experts, dtype=jnp.int32)).astype(jnp.float32)
    gates = jnp.einsum("tke,te->tk", chosen, probs)
    dot_grads = jnp.einsum("td,tkd->tk", incoming, saved_rows, preferred_element_type=jnp.float32)
    weighted = dot_grads * gates
    dense_f = (
        jnp.einsum("tke,tk->te", chosen, weighted) - probs * jnp.sum(weighted, axis=-1)[:, None]
    )
    dense = dense_f.astype(jnp.bfloat16)
    router_term = lax.dot_general(
        dense, router_w, (((1,), (1,)), ((), ())), preferred_element_type=jnp.float32
    )
    back_rows = returned[index_rows].reshape(rows_dev, 2, width).astype(jnp.float32)
    total = (
        incoming.astype(jnp.float32)
        + gates[:, 0, None] * back_rows[:, 0]
        + gates[:, 1, None] * back_rows[:, 1]
        + router_term
    )
    weight_part = lax.dot_general(
        normed_rows, dense, (((0,), (0,)), ((), ())), preferred_element_type=jnp.float32
    )
    return (total.astype(jnp.bfloat16), weight_part)


def on_device(normed, saved_out, expert_grads, routes, router_weight, upstream):
    micro = normed.shape[1]
    rows_dev = normed.shape[2]
    width = normed.shape[3]
    sections = lax.axis_size("pipe")
    section_idx = lax.axis_index("pipe")
    router_w = router_weight[0]
    experts = router_w.shape[1]
    capacity = expert_grads.shape[5]
    slot_rows = slot_index(routes[0].reshape(micro, -1), experts, capacity)
    local_grads = expert_grads[0, :, 0]
    returned_list = []
    for block_num in range(micro):
        received = lax.all_to_all(
            local_grads[block_num], "expert", split_axis=1, concat_axis=0, tiled=True
        )
        returned_list.append(received.reshape(experts * capacity, width))
    returned_all = jnp.stack(returned_list)
    grad_buffer = jnp.zeros((micro, rows_dev, width), jnp.bfloat16)
    weight_sum = jnp.zeros((width, experts), jnp.float32)
    passed = jnp.zeros((rows_dev, width), jnp.bfloat16)
    for tick_num in range(micro + sections - 1):
        if tick_num > 0:
            passed = shifted(passed, "pipe", -1)
        block_num = tick_num - (sections - 1 - section_idx)
        is_active = (block_num >= 0) & (block_num < micro)
        block_idx = jnp.clip(block_num, 0, micro - 1)
        returned = lax.dynamic_index_in_dim(returned_all, block_idx, 0, keepdims=False)
        from_top = lax.dynamic_index_in_dim(upstream, block_idx, 0, keepdims=False)
        incoming = jnp.where(section_idx == sections - 1, from_top, passed)
        new_grad, weight_part = block_grad(
            incoming,
            lax.dynamic_index_in_dim(normed[0], block_idx, 0, keepdims=False),
            lax.dynamic_index_in_dim(saved_out[0], block_idx, 0, keepdims=False),
            lax.dynamic_index_in_dim(routes[0], block_idx, 0, keepdims=False),
            returned,
            lax.dynamic_index_in_dim(slot_rows, block_idx, 0, keepdims=False),
            router_w,
        )
        updated = lax.dynamic_update_index_in_dim(grad_buffer, new_grad, block_idx, 0)
        grad_buffer = jnp.where(is_active, updated, grad_buffer)
        weight_sum = weight_sum + jnp.where(is_active, weight_part, 0.0)
        passed = new_grad
    router_grad = lax.psum(weight_sum / micro, ("expert", "dp"))
    return (grad_buffer[None], router_grad[None])


def solution(mesh):
    in_specs = (
        P("pipe", None, ("expert", "dp"), None),
        P("pipe", None, ("expert", "dp"), None, None),
        P("pipe", None, "dp", "expert", None, None, None),
        P("pipe", None, ("expert", "dp"), None),
        P("pipe", None, None),
        P(None, ("expert", "dp"), None),
    )
    out_specs = (P("pipe", None, ("expert", "dp"), None), P("pipe", None, None))
    return jax.shard_map(
        on_device, mesh=mesh, in_specs=in_specs, out_specs=out_specs, check_vma=False
    )
```

profile of v0, /device:TPU:1, one launch (start us, length us, event | category | flops | bytes accessed | tf_op | source)
XLA Modules:
  0.0 636.1 jit_solution(2353032965511129839)
XLA Ops:
  7.2 4.4 fusion.196
  11.6 2.1 copy.367
  13.7 10.1 %all-to-all-start = ((bf16[1,16,9,4096]{3,2,0,1:T(8,128)(2,1)}), bf16[1,16,9,4096]{3,2,0,1:T(8,128)(2,1)}, u32[]{:S(2)}, u32[]{:S(2)}) async-start(bf16[1,16,9,4096]{3,2,0,1:T(8,128)(2,1)} %bitcast.551), calls=%async_computation | async-start | bytes 4194304 | tf_op jit(solution)/shard_map/all_to_all | solution.py:64
  27.9 2.1 fusion.49
  30.8 3.4 copy.366
  39.4 33.5 %all-to-all-done = bf16[1,16,9,4096]{3,2,0,1:T(8,128)(2,1)} async-done(((bf16[1,16,9,4096]{3,2,0,1:T(8,128)(2,1)}), bf16[1,16,9,4096]{3,2,0,1:T(8,128)(2,1)}, u32[]{:S(2)}, u32[]{:S(2)}) %all-to-all-start) | async-done | bytes 1179680 | tf_op jit(solution)/shard_map/all_to_all | solution.py:64
  72.9 5.0 all-to-all-start.1
  78.8 3.5 copy.365
  82.3 2.1 copy.364
  97.5 29.4 %all-to-all-done.1 = bf16[1,16,9,4096]{3,2,0,1:T(8,128)(2,1)} async-done(((bf16[1,16,9,4096]{3,2,0,1:T(8,128)(2,1)}), bf16[1,16,9,4096]{3,2,0,1:T(8,128)(2,1)}, u32[]{:S(2)}, u32[]{:S(2)}) %all-to-all-start.1) | async-done | bytes 1179680 | tf_op jit(solution)/shard_map/all_to_all | solution.py:64
  126.9 5.0 all-to-all-start.2
  143.3 37.7 %all-to-all-done.2 = bf16[1,16,9,4096]{3,2,0,1:T(8,128)(2,1)} async-done(((bf16[1,16,9,4096]{3,2,0,1:T(8,128)(2,1)}), bf16[1,16,9,4096]{3,2,0,1:T(8,128)(2,1)}, u32[]{:S(2)}, u32[]{:S(2)}) %all-to-all-start.2) | async-done | bytes 1179680 | tf_op jit(solution)/shard_map/all_to_all | solution.py:64
  181.0 5.1 all-to-all-start.3
  188.2 2.6 stack_reshape.12
  190.8 2.7 stack_reshape.13
  193.5 2.6 stack_reshape.14
  196.1 2.5 constant_dynamic-update-slice_fusion.3
  201.4 33.7 %all-to-all-done.3 = bf16[1,16,9,4096]{3,2,0,1:T(8,128)(2,1)} async-done(((bf16[1,16,9,4096]{3,2,0,1:T(8,128)(2,1)}), bf16[1,16,9,4096]{3,2,0,1:T(8,128)(2,1)}, u32[]{:S(2)}, u32[]{:S(2)}) %all-to-all-start.3) | async-done | bytes 1179680 | tf_op jit(solution)/shard_map/all_to_all | solution.py:64
  235.1 2.6 stack_reshape.15
  237.8 2.4 constant_dynamic-update-slice_fusion
  240.2 7.0 %dynamic-slice_bitcast_fusion = (bf16[144,4096]{1,0:T(8,128)(2,1)}, bf16[144,4096]{1,0:T(8,128)(2,1)}, bf16[144,4096]{1,0:T(8,128)(2,1)}, bf16[144,4096]{1,0:T(8...) fusion(bf16[4,144,4096]{2,1,0:T(8,128)(2,1)} %constant_dynamic-update-slice_fusion, ...), kind=kLoop, calls=%fused_computation.28 | loop fusion | bytes 16515100 | tf_op jit(solution)/shard_map/jit(dynamic_index_in_dim)/squeeze | solution.py:78
  247.1 4.1 gather_fusion
  251.3 2.9 reshape.322
  254.2 3.6 fusion.203
  259.1 3.0 bitcast_dynamic-update-slice_fusion
  263.8 4.2 gather_fusion.1
  268.0 2.9 reshape.323
  271.0 4.7 fusion.202
  275.7 4.2 gather_fusion.2
  279.9 2.9 reshape.324
  282.9 4.7 fusion.201
  287.6 4.2 gather_fusion.3
  291.8 3.1 reshape.325
  294.9 4.7 fusion.200
  299.6 4.3 gather_fusion.4
  303.9 2.9 reshape.326
  308.0 2.7 fusion.50
  319.0 3.8 fusion.81
  324.1 3.0 fusion.199
  327.1 4.2 gather_fusion.5
  331.3 3.1 reshape.327
  337.2 2.7 fusion.51
  348.2 3.8 fusion.78
  353.2 2.9 fusion.198
  356.2 4.3 gather_fusion.6
  360.5 2.9 reshape.328
  364.8 2.7 fusion.52
  368.9 1.9 fusion.192
  375.8 3.6 fusion.75
  381.1 2.9 fusion.197
  384.1 1.9 fusion.8
  385.9 4.9 collective-permute-done.3
  392.7 2.1 fusion.53
  395.4 3.7 fusion.72
  400.8 8.6 %collective-permute-done.4 = bf16[48,4096]{1,0:T(8,128)(2,1)S(1)} collective-permute-done((bf16[48,4096]{1,0:T(8,128)(2,1)S(1)}, bf16[48,4096]{1,0:T(8,128)(2,1)S(1)}, u32[]{:S(2)}, u32[]{:S(2)}) %collective-permute-start.4) | collective-permute-done | bytes 393248 | tf_op jit(solution)/shard_map/ppermute | solution.py:10
  411.2 2.7 fusion.54
  421.9 3.6 fusion.69
  427.1 2.7 copy.377
  430.0 4.8 collective-permute-done.5
  436.6 2.7 fusion.55
  440.8 1.8 fusion.189
  447.6 1.9 fusion.3
  449.5 3.5 fusion.66
  453.1 174.1 %all-reduce.2.cloned.1.call-done = f32[1,4096,16]{1,2,0:T(8,128)} async-done(((f32[1,4096,16]{1,2,0:T(8,128)}), f32[1,4096,16]{1,2,0:T(8,128)}) %all-reduce.2.cloned.1.call-update) | async-done | bytes 262160 | tf_op jit(solution)/shard_map/psum | solution.py:94
  (254 shorter events, 100.8 us)
Async XLA Ops:
  7.2 20.7 %copy-start = (bf16[1,4,48,2,4096]{4,3,2,1,0:T(2,128)(2,1)S(1)}, bf16[1,4,48,2,4096]{4,3,2,1,0:T(2,128)(2,1)}, u32[]{:S(2)}) copy-start(bf16[1,4,48,2,4096]{4,3,2,1,0:T(2,128)(2,1)} %param.7) | copy-start | bytes 9437188
  13.7 10.1 %copy-start.43 = (s32[1,4,48,2]{2,3,1,0:T(2,128)S(1)}, s32[1,4,48,2]{2,3,1,0:T(2,128)}, u32[]{:S(2)}) copy-start(s32[1,4,48,2]{2,3,1,0:T(2,128)} %param.9) | copy-start | bytes 4612
  13.7 10.9 %copy-start.1 = (bf16[1,4096,16]{1,2,0:T(8,128)(2,1)S(1)}, bf16[1,4096,16]{1,2,0:T(8,128)(2,1)}, u32[]{:S(2)}) copy-start(bf16[1,4096,16]{1,2,0:T(8,128)(2,1)} %param.10) | copy-start | bytes 393220
  13.7 59.2 %all-to-all-start = ((bf16[1,16,9,4096]{3,2,0,1:T(8,128)(2,1)}), bf16[1,16,9,4096]{3,2,0,1:T(8,128)(2,1)}, u32[]{:S(2)}, u32[]{:S(2)}) async-start(bf16[1,16,9,4096]{3,2,0,1:T(8,128)(2,1)} %bitcast.551), calls=%async_computation | async-start | bytes 4194304 | tf_op jit(solution)/shard_map/all_to_all | solution.py:64
  26.8 3.3 copy-start.47
  34.2 38.7 %copy-start.41 = (s32[4,96]{1,0:T(4,128)}, s32[4,96]{1,0:T(4,128)S(1)}, u32[]{:S(2)}) copy-start(s32[4,96]{1,0:T(4,128)S(1)} %copy.75) | copy-start | bytes 4612
  34.3 38.6 %copy-start.20 = (s32[48,2]{1,0:T(8,128)}, s32[48,2]{1,0:T(8,128)S(1)}, u32[]{:S(2)}) copy-start(s32[48,2]{1,0:T(8,128)S(1)} %copy.79) | copy-start | bytes 1156
  35.5 0.6 copy-start.29
  36.2 41.6 %copy-start.18 = (s32[48,2]{1,0:T(8,128)}, s32[48,2]{1,0:T(8,128)S(1)}, u32[]{:S(2)}) copy-start(s32[48,2]{1,0:T(8,128)S(1)} %copy.82) | copy-start | bytes 1156
  72.9 54.0 %all-to-all-start.1 = ((bf16[1,16,9,4096]{3,2,0,1:T(8,128)(2,1)}), bf16[1,16,9,4096]{3,2,0,1:T(8,128)(2,1)}, u32[]{:S(2)}, u32[]{:S(2)}) async-start(bf16[1,16,9,4096]{3,2,0,1:T(8,128)(2,1)} %bitcast.550), calls=%async_computation.1 | async-start | bytes 4194304 | tf_op jit(solution)/shard_map/all_to_all | solution.py:64
  78.8 3.5 copy-start.7
  86.9 2.8 copy-start.19
  90.5 2.7 copy-start.16
  91.7 0.6 copy-start.23
  93.3 2.7 copy-start.15
  96.2 35.7 %copy-start.14 = (s32[48,2]{1,0:T(8,128)}, s32[48,2]{1,0:T(8,128)S(1)}, u32[]{:S(2)}) copy-start(s32[48,2]{1,0:T(8,128)S(1)} %copy.94) | copy-start | bytes 1156
  97.4 29.5 %copy-start.48 = (f32[48]{0:T(128)}, f32[48]{0:T(128)S(1)}, u32[]{:S(2)}) copy-start(f32[48]{0:T(128)S(1)} %get-tuple-element.93) | copy-start | bytes 580
  126.9 54.0 %all-to-all-start.2 = ((bf16[1,16,9,4096]{3,2,0,1:T(8,128)(2,1)}), bf16[1,16,9,4096]{3,2,0,1:T(8,128)(2,1)}, u32[]{:S(2)}, u32[]{:S(2)}) async-start(bf16[1,16,9,4096]{3,2,0,1:T(8,128)(2,1)} %bitcast.549), calls=%async_computation.2 | async-start | bytes 4194304 | tf_op jit(solution)/shard_map/all_to_all | solution.py:64
  132.2 54.2 %copy-start.44 = (f32[48,2]{0,1:T(2,128)}, f32[48,2]{0,1:T(2,128)S(1)}, u32[]{:S(2)}) copy-start(f32[48,2]{0,1:T(2,128)S(1)} %copy.167) | copy-start | bytes 1156
  180.9 6.0 copy-start.32
  181.0 6.0 copy-start.42
  181.0 6.0 copy-start.57
  181.0 6.0 copy-start.60
  181.0 54.2 %all-to-all-start.3 = ((bf16[1,16,9,4096]{3,2,0,1:T(8,128)(2,1)}), bf16[1,16,9,4096]{3,2,0,1:T(8,128)(2,1)}, u32[]{:S(2)}, u32[]{:S(2)}) async-start(bf16[1,16,9,4096]{3,2,0,1:T(8,128)(2,1)} %bitcast.548), calls=%async_computation.3 | async-start | bytes 4194304 | tf_op jit(solution)/shard_map/all_to_all | solution.py:64
  186.1 441.1 %all-reduce.2.cloned.1.call-start = ((), (), s32[]{:S(2)}) async-start(), calls=%async_computation.4 | async-start | bytes 524288 | tf_op jit(solution)/shard_map/psum | solution.py:94
  196.1 2.5 copy-start.9
  198.6 1.7 copy-start.8
  257.8 1.4 copy-start.61
  257.8 1.4 copy-start.62
  262.1 44.7 %collective-permute-start = (bf16[48,4096]{1,0:T(8,128)(2,1)}, bf16[48,4096]{1,0:T(8,128)(2,1)}, u32[]{:S(2)}, u32[]{:S(2)}) collective-permute-start(bf16[48,4096]{1,0:T(8,128)(2,1)} %get-tuple-element.72), channel_id=1, source_target_pairs={{64,0},{128,64},{192,128},{65,1},{129,65},{193,129},{66,2},{130,66... | collective-permute-start | bytes 1179656 | tf_op jit(solution)/shard_map/ppermute | solution.py:10
  308.0 10.3 %copy-start.30 = (f32[48,16]{0,1:T(8,128)S(1)}, f32[48,16]{0,1:T(8,128)}, u32[]{:S(2)}) copy-start(f32[48,16]{0,1:T(8,128)} %copy-done.29) | copy-start | bytes 9220
  319.0 3.8 copy-start.33
  319.0 5.1 copy-start.4
  322.8 13.2 %collective-permute-start.1 = (bf16[48,4096]{1,0:T(8,128)(2,1)}, bf16[48,4096]{1,0:T(8,128)(2,1)}, u32[]{:S(2)}, u32[]{:S(2)}) collective-permute-start(bf16[48,4096]{1,0:T(8,128)(2,1)} %get-tuple-element.76), channel_id=1, source_target_pairs={{64,0},{128,64},{192,128},{65,1},{129,65},{193,129},{66,2},{130,66... | collective-permute-start | bytes 1179656 | tf_op jit(solution)/shard_map/ppermute | solution.py:10
  337.1 10.3 %copy-start.26 = (f32[48,16]{0,1:T(8,128)S(1)}, f32[48,16]{0,1:T(8,128)}, u32[]{:S(2)}) copy-start(f32[48,16]{0,1:T(8,128)} %copy-done.25) | copy-start | bytes 9220
  348.2 3.8 copy-start.35
  348.2 5.1 copy-start.5
  352.0 11.6 %collective-permute-start.2 = (bf16[48,4096]{1,0:T(8,128)(2,1)}, bf16[48,4096]{1,0:T(8,128)(2,1)}, u32[]{:S(2)}, u32[]{:S(2)}) collective-permute-start(bf16[48,4096]{1,0:T(8,128)(2,1)} %get-tuple-element.80), channel_id=1, source_target_pairs={{64,0},{128,64},{192,128},{65,1},{129,65},{193,129},{66,2},{130,66... | collective-permute-start | bytes 1179656 | tf_op jit(solution)/shard_map/ppermute | solution.py:10
  364.7 10.3 %copy-start.28 = (f32[48,16]{0,1:T(8,128)S(1)}, f32[48,16]{0,1:T(8,128)}, u32[]{:S(2)}) copy-start(f32[48,16]{0,1:T(8,128)} %copy-done.27) | copy-start | bytes 9220
  375.8 3.7 copy-start.37
  375.8 5.3 copy-start.6
  379.4 4.6 copy-start.34
  379.4 11.4 %collective-permute-start.3 = (bf16[48,4096]{1,0:T(8,128)(2,1)S(1)}, bf16[48,4096]{1,0:T(8,128)(2,1)S(1)}, u32[]{:S(2)}, u32[]{:S(2)}) collective-permute-start(bf16[48,4096]{1,0:T(8,128)(2,1)S(1)} %get-tuple-element.84), channel_id=1, source_target_pairs={{64,0},{128,64},{192,128},{65,1},{129,65},{193,129},{66,2},{130,66... | collective-permute-start | bytes 1179656 | tf_op jit(solution)/shard_map/ppermute | solution.py:10
  390.8 0.7 copy-start.12
  392.6 2.3 copy-start.46
  392.6 2.4 copy-start.17
  392.7 2.6 copy-start.24
  392.7 2.6 copy-start.52
  392.7 2.7 copy-start.58
  392.7 2.7 copy-start.59
  395.3 3.7 copy-start.39
  395.3 5.0 copy-start.2
  395.4 5.0 copy-start.13
  395.4 5.0 copy-start.36
  395.4 5.2 copy-start.38
  399.1 10.3 %collective-permute-start.4 = (bf16[48,4096]{1,0:T(8,128)(2,1)S(1)}, bf16[48,4096]{1,0:T(8,128)(2,1)S(1)}, u32[]{:S(2)}, u32[]{:S(2)}) collective-permute-start(bf16[48,4096]{1,0:T(8,128)(2,1)S(1)} %get-tuple-element.88), channel_id=1, source_target_pairs={{64,0},{128,64},{192,128},{65,1},{129,65},{193,129},{66,2},{130,66... | collective-permute-start | bytes 1179656 | tf_op jit(solution)/shard_map/ppermute | solution.py:10
  409.4 0.7 copy-start.11
  411.2 10.1 %copy-start.22 = (f32[48,16]{0,1:T(8,128)S(1)}, f32[48,16]{0,1:T(8,128)}, u32[]{:S(2)}) copy-start(f32[48,16]{0,1:T(8,128)} %copy-done.21) | copy-start | bytes 9220
  421.9 4.9 copy-start.3
  421.9 5.0 copy-start.40
  425.6 9.2 %collective-permute-start.5 = (bf16[48,4096]{1,0:T(8,128)(2,1)S(1)}, bf16[48,4096]{1,0:T(8,128)(2,1)S(1)}, u32[]{:S(2)}, u32[]{:S(2)}) collective-permute-start(bf16[48,4096]{1,0:T(8,128)(2,1)S(1)} %get-tuple-element.92), channel_id=1, source_target_pairs={{64,0},{128,64},{192,128},{65,1},{129,65},{193,129},{66,2},{130,66... | collective-permute-start | bytes 1179656 | tf_op jit(solution)/shard_map/ppermute | solution.py:10
  434.8 0.8 copy-start.10
  436.6 4.2 copy-start.45
  436.6 10.3 %copy-start.49 = (f32[48]{0:T(128)S(1)}, f32[48]{0:T(128)}, u32[]{:S(2)}) copy-start(f32[48]{0:T(128)} %copy-done.48) | copy-start | bytes 580
  (10 other events, 6.0 us)
Sparse Core Ops, SparseCore 0:
  449.7 177.4 all-reduce.1
where the time goes:
time: 646 us; the launch traced here: 636 us
  waiting for transfers between devices  328 us (51%)
  local copies, waits for them, and re-layouts  165 us (26%)
  matrix products  57.4 us (9%)
  other arithmetic  35.6 us (6%)
  starting transfers between devices  33.9 us (5%)
  between operations  15.2 us (2%)
    psum x1, waiting for transfers between devices, on_device(): router_grad = lax.psum(weight_sum / micro, ('expert', 'dp'))  174 us
    all_to_all x4, waiting for transfers between devices, on_device(): lax.all_to_all(local_grads[block_num], 'expert', split_axis=1, concat_axi...  134 us
    unnamed x150, local copies, waits for them, and re-layouts  34.3 us
    gather x7, local copies, waits for them, and re-layouts, block_grad(): returned[index_rows].reshape(rows_dev, 2, width).astype(jnp.float32)  29.6 us
    slice x7, local copies, waits for them, and re-layouts, block_grad(): back_rows[:, 0]  26.5 us
    all_to_all x4, starting transfers between devices, on_device(): lax.all_to_all(local_grads[block_num], 'expert', split_axis=1, concat_axi...  25.2 us
    dot_general x7, matrix products, block_grad(): lax.dot_general(dense, router_w, (((1,), (1,)), ((), ())), preferred_elem...  25 us
    convert_element_type x7, local copies, waits for them, and re-layouts, block_grad(): returned[index_rows].reshape(rows_dev, 2, width).astype(jnp.float32)  20.9 us
  transfers between devices with their start and end apart: 11, of which 10 were waited for; matrix products, arithmetic and copies ran while one was open for 21% of the time, Pallas kernels for 0%

commit v1 on v0

--- a/solution.py
+++ b/solution.py
@@ -2,6 +2,7 @@
 import jax.numpy as jnp
 from jax import lax
 from jax.sharding import PartitionSpec as P
+from jax.lax import psum
 
 
 def shifted(block, axis, distance):
@@ -91,7 +92,11 @@
         grad_buffer = jnp.where(is_active, updated, grad_buffer)
         weight_sum = weight_sum + jnp.where(is_active, weight_part, 0.0)
         passed = new_grad
-    router_grad = lax.psum(weight_sum / micro, ("expert", "dp"))
+
+    def record_direct(mine):
+        return psum(psum(mine, axis_name="expert"), "dp")
+
+    router_grad = record_direct(weight_sum / micro)
     return (grad_buffer[None], router_grad[None])
 
 

time: 646 us -> 619 us (0.958)
  waiting for transfers between devices: 328 us -> 301 us
    psum x1 -> x2, waiting for transfers between devices: 174 us -> 147 us  [record_direct(): return psum(psum(mine, axis_name='expert'), 'dp')]
    unnamed x150 -> x152, local copies, waits for them, and re-layouts: 34.3 us -> 33.4 us
  transfers between devices with their start and end apart: 11 -> 12, of which waited for: 10 -> 10; matrix products, arithmetic and copies ran while one was open for 21% -> 22% of each run, Pallas kernels for 0% -> 0%
where the time goes in v1:
time: 619 us; the launch traced here: 608 us
  waiting for transfers between devices  301 us (49%)
  local copies, waits for them, and re-layouts  164 us (26%)
  matrix products  57.5 us (9%)
  other arithmetic  35.8 us (6%)
  starting transfers between devices  33.8 us (5%)
  between operations  15.3 us (2%)
    psum x2, waiting for transfers between devices, record_direct(): return psum(psum(mine, axis_name='expert'), 'dp')  147 us
    all_to_all x4, waiting for transfers between devices, on_device(): lax.all_to_all(local_grads[block_num], 'expert', split_axis=1, concat_axi...  134 us
    unnamed x152, local copies, waits for them, and re-layouts  33.4 us
    gather x7, local copies, waits for them, and re-layouts, block_grad(): returned[index_rows].reshape(rows_dev, 2, width).astype(jnp.float32)  29.5 us
    slice x7, local copies, waits for them, and re-layouts, block_grad(): back_rows[:, 0]  26.5 us
    all_to_all x4, starting transfers between devices, on_device(): lax.all_to_all(local_grads[block_num], 'expert', split_axis=1, concat_axi...  25.2 us
    dot_general x7, matrix products, block_grad(): lax.dot_general(dense, router_w, (((1,), (1,)), ((), ())), preferred_elem...  25.1 us
    convert_element_type x7, local copies, waits for them, and re-layouts, block_grad(): returned[index_rows].reshape(rows_dev, 2, width).astype(jnp.float32)  20.9 us
  transfers between devices with their start and end apart: 12, of which 10 were waited for; matrix products, arithmetic and copies ran while one was open for 22% of the time, Pallas kernels for 0%

profile of v1, /device:TPU:1, one launch (start us, length us, event | category | flops | bytes accessed | tf_op | source)
XLA Modules:
  0.0 608.1 jit_solution(5254150858016762186)
XLA Ops:
  7.2 4.4 fusion.195
  11.6 2.1 copy.367
  13.7 10.1 %all-to-all-start = ((bf16[1,16,9,4096]{3,2,0,1:T(8,128)(2,1)}), bf16[1,16,9,4096]{3,2,0,1:T(8,128)(2,1)}, u32[]{:S(2)}, u32[]{:S(2)}) async-start(bf16[1,16,9,4096]{3,2,0,1:T(8,128)(2,1)} %bitcast.550), calls=%async_computation | async-start | bytes 4194304 | tf_op jit(solution)/shard_map/all_to_all | solution.py:65
  27.8 2.1 fusion.48
  30.7 3.4 copy.366
  39.3 33.5 %all-to-all-done = bf16[1,16,9,4096]{3,2,0,1:T(8,128)(2,1)} async-done(((bf16[1,16,9,4096]{3,2,0,1:T(8,128)(2,1)}), bf16[1,16,9,4096]{3,2,0,1:T(8,128)(2,1)}, u32[]{:S(2)}, u32[]{:S(2)}) %all-to-all-start) | async-done | bytes 1179680 | tf_op jit(solution)/shard_map/all_to_all | solution.py:65
  72.9 5.0 all-to-all-start.1
  78.7 3.5 copy.365
  82.3 2.1 copy.364
  97.5 29.4 %all-to-all-done.1 = bf16[1,16,9,4096]{3,2,0,1:T(8,128)(2,1)} async-done(((bf16[1,16,9,4096]{3,2,0,1:T(8,128)(2,1)}), bf16[1,16,9,4096]{3,2,0,1:T(8,128)(2,1)}, u32[]{:S(2)}, u32[]{:S(2)}) %all-to-all-start.1) | async-done | bytes 1179680 | tf_op jit(solution)/shard_map/all_to_all | solution.py:65
  126.9 5.0 all-to-all-start.2
  143.5 37.5 %all-to-all-done.2 = bf16[1,16,9,4096]{3,2,0,1:T(8,128)(2,1)} async-done(((bf16[1,16,9,4096]{3,2,0,1:T(8,128)(2,1)}), bf16[1,16,9,4096]{3,2,0,1:T(8,128)(2,1)}, u32[]{:S(2)}, u32[]{:S(2)}) %all-to-all-start.2) | async-done | bytes 1179680 | tf_op jit(solution)/shard_map/all_to_all | solution.py:65
  180.9 5.1 all-to-all-start.3
  188.1 2.6 stack_reshape.12
  190.7 2.6 stack_reshape.13
  193.4 2.6 stack_reshape.14
  196.0 2.5 constant_dynamic-update-slice_fusion.3
  201.3 33.8 %all-to-all-done.3 = bf16[1,16,9,4096]{3,2,0,1:T(8,128)(2,1)} async-done(((bf16[1,16,9,4096]{3,2,0,1:T(8,128)(2,1)}), bf16[1,16,9,4096]{3,2,0,1:T(8,128)(2,1)}, u32[]{:S(2)}, u32[]{:S(2)}) %all-to-all-start.3) | async-done | bytes 1179680 | tf_op jit(solution)/shard_map/all_to_all | solution.py:65
  235.1 2.6 stack_reshape.15
  237.7 2.4 constant_dynamic-update-slice_fusion
  240.1 7.0 %dynamic-slice_bitcast_fusion = (bf16[144,4096]{1,0:T(8,128)(2,1)}, bf16[144,4096]{1,0:T(8,128)(2,1)}, bf16[144,4096]{1,0:T(8,128)(2,1)}, bf16[144,4096]{1,0:T(8...) fusion(bf16[4,144,4096]{2,1,0:T(8,128)(2,1)} %constant_dynamic-update-slice_fusion, ...), kind=kLoop, calls=%fused_computation.27 | loop fusion | bytes 16515100 | tf_op jit(solution)/shard_map/jit(dynamic_index_in_dim)/squeeze | solution.py:79
  247.1 4.1 gather_fusion
  251.2 2.9 reshape.322
  254.2 3.6 fusion.202
  259.1 3.0 bitcast_dynamic-update-slice_fusion
  263.8 4.2 gather_fusion.1
  268.0 2.9 reshape.323
  271.0 4.7 fusion.201
  275.7 4.2 gather_fusion.2
  279.9 2.9 reshape.324
  282.9 4.7 fusion.200
  287.6 4.2 gather_fusion.3
  291.8 3.1 reshape.325
  296.1 2.7 fusion.49
  307.0 3.8 fusion.80
  312.1 3.0 fusion.199
  315.1 4.3 gather_fusion.4
  319.4 2.9 reshape.326
  325.2 2.7 fusion.50
  329.3 1.9 fusion.192
  336.2 3.8 fusion.77
  341.3 2.9 fusion.198
  344.2 4.2 gather_fusion.5
  348.5 3.1 reshape.327
  352.8 2.7 fusion.51
  357.0 1.8 fusion.191
  363.8 3.8 fusion.74
  368.9 3.0 fusion.197
  371.9 4.2 gather_fusion.6
  376.1 2.9 reshape.328
  379.0 1.9 fusion.7
  382.1 2.1 fusion.52
  384.8 3.6 fusion.71
  390.4 10.2 %collective-permute-done.4 = bf16[48,4096]{1,0:T(8,128)(2,1)S(1)} collective-permute-done((bf16[48,4096]{1,0:T(8,128)(2,1)S(1)}, bf16[48,4096]{1,0:T(8,128)(2,1)S(1)}, u32[]{:S(2)}, u32[]{:S(2)}) %collective-permute-start.4) | collective-permute-done | bytes 393248 | tf_op jit(solution)/shard_map/ppermute | solution.py:11
  402.4 2.7 fusion.53
  413.3 3.6 fusion.68
  418.6 8.4 %collective-permute-done.5 = bf16[48,4096]{1,0:T(8,128)(2,1)S(1)} collective-permute-done((bf16[48,4096]{1,0:T(8,128)(2,1)S(1)}, bf16[48,4096]{1,0:T(8,128)(2,1)S(1)}, u32[]{:S(2)}, u32[]{:S(2)}) %collective-permute-start.5) | collective-permute-done | bytes 393248 | tf_op jit(solution)/shard_map/ppermute | solution.py:11
  428.8 2.7 fusion.54
  439.6 1.9 fusion.2
  441.5 4.7 fusion.196
  446.2 2.7 copy.377
  448.9 102.8 %all-reduce.3.cloned.1.call-done = f32[4096,16]{0,1:T(8,128)} async-done(((f32[4096,16]{0,1:T(8,128)}), f32[4096,16]{0,1:T(8,128)}) %all-reduce.3.cloned.1.call-update) | async-done | bytes 262160 | tf_op jit(solution)/shard_map/psum | solution.py:97
  551.8 3.5 fusion.65
  555.3 43.9 %all-reduce.5.cloned.1.call-done = f32[1,4096,16]{1,2,0:T(8,128)} async-done(((f32[1,4096,16]{1,2,0:T(8,128)}), f32[1,4096,16]{1,2,0:T(8,128)}) %all-reduce.5.cloned.1.call-update) | async-done | bytes 262160 | tf_op jit(solution)/shard_map/psum | solution.py:97
  (259 shorter events, 100.2 us)
Async XLA Ops:
  7.2 20.6 %copy-start = (bf16[1,4,48,2,4096]{4,3,2,1,0:T(2,128)(2,1)S(1)}, bf16[1,4,48,2,4096]{4,3,2,1,0:T(2,128)(2,1)}, u32[]{:S(2)}) copy-start(bf16[1,4,48,2,4096]{4,3,2,1,0:T(2,128)(2,1)} %param.7) | copy-start | bytes 9437188
  13.7 10.1 %copy-start.42 = (s32[1,4,48,2]{2,3,1,0:T(2,128)S(1)}, s32[1,4,48,2]{2,3,1,0:T(2,128)}, u32[]{:S(2)}) copy-start(s32[1,4,48,2]{2,3,1,0:T(2,128)} %param.9) | copy-start | bytes 4612
  13.7 10.9 %copy-start.1 = (bf16[1,4096,16]{1,2,0:T(8,128)(2,1)S(1)}, bf16[1,4096,16]{1,2,0:T(8,128)(2,1)}, u32[]{:S(2)}) copy-start(bf16[1,4096,16]{1,2,0:T(8,128)(2,1)} %param.10) | copy-start | bytes 393220
  13.7 59.2 %all-to-all-start = ((bf16[1,16,9,4096]{3,2,0,1:T(8,128)(2,1)}), bf16[1,16,9,4096]{3,2,0,1:T(8,128)(2,1)}, u32[]{:S(2)}, u32[]{:S(2)}) async-start(bf16[1,16,9,4096]{3,2,0,1:T(8,128)(2,1)} %bitcast.550), calls=%async_computation | async-start | bytes 4194304 | tf_op jit(solution)/shard_map/all_to_all | solution.py:65
  26.8 3.3 copy-start.46
  34.1 38.7 %copy-start.40 = (s32[4,96]{1,0:T(4,128)}, s32[4,96]{1,0:T(4,128)S(1)}, u32[]{:S(2)}) copy-start(s32[4,96]{1,0:T(4,128)S(1)} %copy.75) | copy-start | bytes 4612
  34.2 38.6 %copy-start.19 = (s32[48,2]{1,0:T(8,128)}, s32[48,2]{1,0:T(8,128)S(1)}, u32[]{:S(2)}) copy-start(s32[48,2]{1,0:T(8,128)S(1)} %copy.79) | copy-start | bytes 1156
  36.2 41.6 %copy-start.17 = (s32[48,2]{1,0:T(8,128)}, s32[48,2]{1,0:T(8,128)S(1)}, u32[]{:S(2)}) copy-start(s32[48,2]{1,0:T(8,128)S(1)} %copy.82) | copy-start | bytes 1156
  72.9 54.0 %all-to-all-start.1 = ((bf16[1,16,9,4096]{3,2,0,1:T(8,128)(2,1)}), bf16[1,16,9,4096]{3,2,0,1:T(8,128)(2,1)}, u32[]{:S(2)}, u32[]{:S(2)}) async-start(bf16[1,16,9,4096]{3,2,0,1:T(8,128)(2,1)} %bitcast.549), calls=%async_computation.1 | async-start | bytes 4194304 | tf_op jit(solution)/shard_map/all_to_all | solution.py:65
  78.7 3.5 copy-start.7
  86.9 2.8 copy-start.18
  90.4 2.8 copy-start.15
  93.3 2.8 copy-start.14
  96.2 35.7 %copy-start.13 = (s32[48,2]{1,0:T(8,128)}, s32[48,2]{1,0:T(8,128)S(1)}, u32[]{:S(2)}) copy-start(s32[48,2]{1,0:T(8,128)S(1)} %copy.94) | copy-start | bytes 1156
  97.4 29.5 %copy-start.47 = (f32[48]{0:T(128)}, f32[48]{0:T(128)S(1)}, u32[]{:S(2)}) copy-start(f32[48]{0:T(128)S(1)} %get-tuple-element.93) | copy-start | bytes 580
  126.9 54.0 %all-to-all-start.2 = ((bf16[1,16,9,4096]{3,2,0,1:T(8,128)(2,1)}), bf16[1,16,9,4096]{3,2,0,1:T(8,128)(2,1)}, u32[]{:S(2)}, u32[]{:S(2)}) async-start(bf16[1,16,9,4096]{3,2,0,1:T(8,128)(2,1)} %bitcast.548), calls=%async_computation.2 | async-start | bytes 4194304 | tf_op jit(solution)/shard_map/all_to_all | solution.py:65
  132.2 54.2 %copy-start.43 = (f32[48,2]{0,1:T(2,128)}, f32[48,2]{0,1:T(2,128)S(1)}, u32[]{:S(2)}) copy-start(f32[48,2]{0,1:T(2,128)S(1)} %copy.167) | copy-start | bytes 1156
  180.9 6.0 copy-start.31
  180.9 6.0 copy-start.41
  180.9 6.0 copy-start.56
  180.9 6.0 copy-start.61
  180.9 54.2 %all-to-all-start.3 = ((bf16[1,16,9,4096]{3,2,0,1:T(8,128)(2,1)}), bf16[1,16,9,4096]{3,2,0,1:T(8,128)(2,1)}, u32[]{:S(2)}, u32[]{:S(2)}) async-start(bf16[1,16,9,4096]{3,2,0,1:T(8,128)(2,1)} %bitcast.547), calls=%async_computation.3 | async-start | bytes 4194304 | tf_op jit(solution)/shard_map/all_to_all | solution.py:65
  186.1 365.7 %all-reduce.3.cloned.1.call-start = ((), (), s32[]{:S(2)}) async-start(), calls=%async_computation.4 | async-start | bytes 524288 | tf_op jit(solution)/shard_map/psum | solution.py:97
  196.0 2.5 copy-start.9
  198.5 1.7 copy-start.8
  257.7 1.4 copy-start.62
  257.7 1.4 copy-start.63
  262.1 32.8 %collective-permute-start = (bf16[48,4096]{1,0:T(8,128)(2,1)}, bf16[48,4096]{1,0:T(8,128)(2,1)}, u32[]{:S(2)}, u32[]{:S(2)}) collective-permute-start(bf16[48,4096]{1,0:T(8,128)(2,1)} %get-tuple-element.72), channel_id=1, source_target_pairs={{64,0},{128,64},{192,128},{65,1},{129,65},{193,129},{66,2},{130,66... | collective-permute-start | bytes 1179656 | tf_op jit(solution)/shard_map/ppermute | solution.py:11
  296.0 10.3 %copy-start.29 = (f32[48,16]{0,1:T(8,128)S(1)}, f32[48,16]{0,1:T(8,128)}, u32[]{:S(2)}) copy-start(f32[48,16]{0,1:T(8,128)} %copy-done.28) | copy-start | bytes 9220
  307.0 3.8 copy-start.32
  307.0 5.1 copy-start.4
  310.8 13.2 %collective-permute-start.1 = (bf16[48,4096]{1,0:T(8,128)(2,1)}, bf16[48,4096]{1,0:T(8,128)(2,1)}, u32[]{:S(2)}, u32[]{:S(2)}) collective-permute-start(bf16[48,4096]{1,0:T(8,128)(2,1)} %get-tuple-element.76), channel_id=1, source_target_pairs={{64,0},{128,64},{192,128},{65,1},{129,65},{193,129},{66,2},{130,66... | collective-permute-start | bytes 1179656 | tf_op jit(solution)/shard_map/ppermute | solution.py:11
  325.2 10.3 %copy-start.25 = (f32[48,16]{0,1:T(8,128)S(1)}, f32[48,16]{0,1:T(8,128)}, u32[]{:S(2)}) copy-start(f32[48,16]{0,1:T(8,128)} %copy-done.24) | copy-start | bytes 9220
  336.2 3.8 copy-start.34
  336.2 5.1 copy-start.5
  340.0 11.7 %collective-permute-start.2 = (bf16[48,4096]{1,0:T(8,128)(2,1)}, bf16[48,4096]{1,0:T(8,128)(2,1)}, u32[]{:S(2)}, u32[]{:S(2)}) collective-permute-start(bf16[48,4096]{1,0:T(8,128)(2,1)} %get-tuple-element.80), channel_id=1, source_target_pairs={{64,0},{128,64},{192,128},{65,1},{129,65},{193,129},{66,2},{130,66... | collective-permute-start | bytes 1179656 | tf_op jit(solution)/shard_map/ppermute | solution.py:11
  352.8 10.3 %copy-start.27 = (f32[48,16]{0,1:T(8,128)S(1)}, f32[48,16]{0,1:T(8,128)}, u32[]{:S(2)}) copy-start(f32[48,16]{0,1:T(8,128)} %copy-done.26) | copy-start | bytes 9220
  363.8 3.8 copy-start.36
  363.8 5.1 copy-start.6
  367.6 13.3 %collective-permute-start.3 = (bf16[48,4096]{1,0:T(8,128)(2,1)}, bf16[48,4096]{1,0:T(8,128)(2,1)}, u32[]{:S(2)}, u32[]{:S(2)}) collective-permute-start(bf16[48,4096]{1,0:T(8,128)(2,1)} %get-tuple-element.84), channel_id=1, source_target_pairs={{64,0},{128,64},{192,128},{65,1},{129,65},{193,129},{66,2},{130,66... | collective-permute-start | bytes 1179656 | tf_op jit(solution)/shard_map/ppermute | solution.py:11
  376.1 2.9 copy-start.33
  382.1 2.3 copy-start.45
  382.1 2.4 copy-start.16
  382.1 2.6 copy-start.23
  382.1 2.6 copy-start.51
  382.1 2.7 copy-start.59
  382.1 2.7 copy-start.60
  384.7 3.7 copy-start.38
  384.8 5.2 copy-start.2
  384.8 5.2 copy-start.12
  384.8 5.2 copy-start.35
  384.8 5.4 copy-start.37
  388.5 12.1 %collective-permute-start.4 = (bf16[48,4096]{1,0:T(8,128)(2,1)S(1)}, bf16[48,4096]{1,0:T(8,128)(2,1)S(1)}, u32[]{:S(2)}, u32[]{:S(2)}) collective-permute-start(bf16[48,4096]{1,0:T(8,128)(2,1)S(1)} %get-tuple-element.88), channel_id=1, source_target_pairs={{64,0},{128,64},{192,128},{65,1},{129,65},{193,129},{66,2},{130,66... | collective-permute-start | bytes 1179656 | tf_op jit(solution)/shard_map/ppermute | solution.py:11
  400.6 0.8 copy-start.11
  402.4 10.1 %copy-start.21 = (f32[48,16]{0,1:T(8,128)S(1)}, f32[48,16]{0,1:T(8,128)}, u32[]{:S(2)}) copy-start(f32[48,16]{0,1:T(8,128)} %copy-done.20) | copy-start | bytes 9220
  413.3 4.9 copy-start.3
  413.3 5.0 copy-start.39
  416.9 10.0 %collective-permute-start.5 = (bf16[48,4096]{1,0:T(8,128)(2,1)S(1)}, bf16[48,4096]{1,0:T(8,128)(2,1)S(1)}, u32[]{:S(2)}, u32[]{:S(2)}) collective-permute-start(bf16[48,4096]{1,0:T(8,128)(2,1)S(1)} %get-tuple-element.92), channel_id=1, source_target_pairs={{64,0},{128,64},{192,128},{65,1},{129,65},{193,129},{66,2},{130,66... | collective-permute-start | bytes 1179656 | tf_op jit(solution)/shard_map/ppermute | solution.py:11
  427.0 0.7 copy-start.10
  428.8 4.1 copy-start.44
  428.8 10.1 %copy-start.48 = (f32[48]{0:T(128)S(1)}, f32[48]{0:T(128)}, u32[]{:S(2)}) copy-start(f32[48]{0:T(128)} %copy-done.47) | copy-start | bytes 580
  441.5 157.7 %all-reduce.5.cloned.1.call-start = ((), (), s32[]{:S(2)}) async-start(), calls=%async_computation.5 | async-start | bytes 524288 | tf_op jit(solution)/shard_map/psum | solution.py:97
  446.2 105.5 %copy-start.57 = (f32[48]{0:T(128)S(1)}, f32[48]{0:T(128)}, u32[]{:S(2)}) copy-start(f32[48]{0:T(128)} %get-tuple-element.55) | copy-start | bytes 580
  446.2 105.5 %copy-start.58 = (f32[48]{0:T(128)S(1)}, f32[48]{0:T(128)}, u32[]{:S(2)}) copy-start(f32[48]{0:T(128)} %get-tuple-element.56) | copy-start | bytes 580
  (12 other events, 7.2 us)
Sparse Core Ops, SparseCore 0:
  441.6 110.0 all-reduce.2
  554.2 44.9 all-reduce.4
